TPU v7x, 32 devices: a whole 2x2x4 slice. The times are simulated.
32 devices in a mesh: img: 8 (over y, x, core), head: 4 (over z).
Axes of the slice: x: 2, y: 2, z: 4, core: 2. Of those that a mesh axis runs over, the one named last changes fastest.
Arguments:
- latents: bfloat16 [192, 64, 1024], P('img'), may hold values from -6 to 6
- media: bfloat16 [192, 256, 1024], P('img'), may hold values from -6 to 6
- valid_counts: int32 [192], P('img'), may hold values from 160 to 256, as said below
- w_query: bfloat16 [1024, 512], P(None, 'head'), may hold values from -0.1875 to 0.1875
- w_key: bfloat16 [1024, 512], P(None, 'head'), may hold values from -0.1875 to 0.1875
- w_value: bfloat16 [1024, 512], P(None, 'head'), may hold values from -0.1875 to 0.1875
- w_out: bfloat16 [1024, 512], P(None, 'head'), may hold values from -2 to 2
- w_up: bfloat16 [1024, 4096], P(None, 'head'), may hold values from -0.1875 to 0.1875
- w_down: bfloat16 [1024, 4096], P(None, 'head'), may hold values from -0.09375 to 0.09375
- norm_gains: float32 [3, 1024], replicated, may hold values from 0.5 to 1.5
- norm_biases: float32 [3, 1024], replicated, may hold values from -1.8 to 1.8
- cotangent: bfloat16 [192, 64, 1024], P('img'), may hold values from -6 to 6
Outputs:
- latents_out: bfloat16 [192, 64, 1024], P('img')
- latents_grad: bfloat16 [192, 64, 1024], P('img', 'head')
- media_grad: bfloat16 [192, 256, 1024], P('img', 'head')
- w_query_grad: float32 [1024, 512], P('img', 'head')
- w_key_grad: float32 [1024, 512], P('img', 'head')
- w_value_grad: float32 [1024, 512], P('img', 'head')
- w_out_grad: float32 [1024, 512], P('img', 'head')
- w_up_grad: float32 [1024, 4096], P('img', 'head')
- w_down_grad: float32 [1024, 4096], P('img', 'head')
- norm_gains_grad: float32 [3, 1024], P(None, ('img', 'head'))
- norm_biases_grad: float32 [3, 1024], P(None, ('img', 'head'))
Inputs may be any that keep to these rules, and one draw needn't show every extreme that they name: An image's valid patch keys are its first valid_counts patches; some image has exactly 256 and some exactly 160.
All inputs are finite; a program needn't handle non-finite values.
Results may differ from a plain program's by a relative error of at most 0.018.
Values may be sent and summed in bfloat16 or wider, within the bound.
No kernel may reach another device: no remote copies, remote signals or barrier semaphores. Data moves between devices by JAX's collectives and lax.ppermute only.
A program may use at most 192 MiB of HBM per device.

v0:
```python
import jax
import jax.numpy as jnp
from jax import lax
from jax.sharding import PartitionSpec as P

HEAD_DIM = 64


epsilon = 1e-05


def layer_norm(values, gain_row, bias_row):
    center = jnp.mean(values, axis=-1, keepdims=True)
    centered = values - center
    spread = jnp.mean(centered * centered, axis=-1, keepdims=True)
    return centered * lax.rsqrt(spread + epsilon) * gain_row + bias_row


def exact_gelu(values):
    return jax.nn.gelu(values, approximate=False)


def rows_share(values, member, count):
    return lax.dynamic_slice_in_dim(values, member * count, count, 1)


def body(
    latents,
    media,
    valid_counts,
    w_query,
    w_key,
    w_value,
    w_out,
    w_up,
    w_down,
    norm_gains,
    norm_biases,
    cotangent,
):
    groups = lax.axis_size("head")
    member = lax.axis_index("head")
    images, patches, model_width = media.shape
    latent_rows = latents.shape[1]
    share_rows = latent_rows // groups
    local_width = w_query.shape[1]
    local_heads = local_width // HEAD_DIM
    score_scale = HEAD_DIM ** (-0.5)
    latent_in = latents.astype(jnp.float32)
    media_in = media.astype(jnp.float32)
    media_normed = layer_norm(media_in, norm_gains[0], norm_biases[0]).astype(jnp.bfloat16)
    latent_normed = layer_norm(latent_in, norm_gains[1], norm_biases[1]).astype(jnp.bfloat16)
    joint_weight = jnp.concatenate([w_query, w_key, w_value], axis=1)
    media_kv = jnp.einsum(
        "ipd,de->ipe",
        media_normed,
        joint_weight[:, local_width:],
        preferred_element_type=jnp.float32,
    ).astype(jnp.bfloat16)
    latent_qkv = jnp.einsum(
        "ild,de->ile", latent_normed, joint_weight, preferred_element_type=jnp.float32
    ).astype(jnp.bfloat16)
    queries = latent_qkv[..., :local_width].reshape(images, latent_rows, local_heads, HEAD_DIM)
    key_rows = jnp.concatenate(
        [media_kv[..., :local_width], latent_qkv[..., local_width : 2 * local_width]], axis=1
    )
    key_rows = key_rows.reshape(images, patches + latent_rows, local_heads, HEAD_DIM)
    value_rows = jnp.concatenate(
        [media_kv[..., local_width:], latent_qkv[..., 2 * local_width :]], axis=1
    )
    value_rows = value_rows.reshape(images, patches + latent_rows, local_heads, HEAD_DIM)
    positions = lax.iota(jnp.int32, patches + latent_rows)
    allowed = (positions[None, :] < valid_counts[:, None]) | (positions[None, :] >= patches)
    scores = (
        jnp.einsum("ilhe,ikhe->ihlk", queries, key_rows, preferred_element_type=jnp.float32)
        * score_scale
    )
    scores = jnp.where(allowed[:, None, None, :], scores, -1e30)
    attention = jax.nn.softmax(scores, axis=-1)
    attention_low = attention.astype(jnp.bfloat16)
    attended = jnp.einsum(
        "ihlk,ikhe->ilhe", attention_low, value_rows, preferred_element_type=jnp.float32
    )
    attended = attended.astype(jnp.bfloat16).reshape(images, latent_rows, local_width)
    attn_part = jnp.einsum("ile,de->ild", attended, w_out, preferred_element_type=jnp.float32)
    residual = latent_in + lax.psum(attn_part.astype(jnp.bfloat16), "head").astype(jnp.float32)
    ffn_low = layer_norm(residual, norm_gains[2], norm_biases[2]).astype(jnp.bfloat16)
    pre_act = jnp.einsum("ild,df->ilf", ffn_low, w_up, preferred_element_type=jnp.float32)
    hidden, gelu_puller = jax.vjp(exact_gelu, pre_act)
    hidden_low = hidden.astype(jnp.bfloat16)
    mlp_part = jnp.einsum("ilf,df->ild", hidden_low, w_down, preferred_element_type=jnp.float32)
    latents_out = (
        residual + lax.psum(mlp_part.astype(jnp.bfloat16), "head").astype(jnp.float32)
    ).astype(jnp.bfloat16)
    upstream = cotangent.astype(jnp.float32)
    grad_down = jnp.einsum("ild,ilf->df", cotangent, hidden_low, preferred_element_type=jnp.float32)
    grad_hidden = jnp.einsum("ild,df->ilf", cotangent, w_down, preferred_element_type=jnp.float32)
    grad_pre = gelu_puller(grad_hidden)[0].astype(jnp.bfloat16)
    grad_up = jnp.einsum("ild,ilf->df", ffn_low, grad_pre, preferred_element_type=jnp.float32)
    grad_ffn_part = jnp.einsum("ilf,df->ild", grad_pre, w_up, preferred_element_type=jnp.float32)
    grad_ffn = lax.psum(grad_ffn_part.astype(jnp.bfloat16), "head").astype(jnp.float32)
    norm_puller = jax.vjp(layer_norm, residual, norm_gains[2], norm_biases[2])[1]
    grad_from_norm, gain_ffn, bias_ffn = norm_puller(grad_ffn)
    grad_residual = upstream + grad_from_norm
    grad_low = grad_residual.astype(jnp.bfloat16)
    grad_residual_share = rows_share(grad_residual, member, share_rows)
    gain_ffn = gain_ffn / groups
    bias_ffn = bias_ffn / groups
    grad_wout = jnp.einsum("ild,ile->de", grad_low, attended, preferred_element_type=jnp.float32)
    grad_attended = jnp.einsum("ild,de->ile", grad_low, w_out, preferred_element_type=jnp.float32)
    grad_attended = grad_attended.astype(jnp.bfloat16).reshape(
        images, latent_rows, local_heads, HEAD_DIM
    )
    grad_values = jnp.einsum(
        "ihlk,ilhe->ikhe", attention_low, grad_attended, preferred_element_type=jnp.float32
    )
    grad_attention = jnp.einsum(
        "ilhe,ikhe->ihlk", grad_attended, value_rows, preferred_element_type=jnp.float32
    )
    row_total = jnp.sum(attention * grad_attention, axis=-1, keepdims=True)
    grad_scores = (attention * (grad_attention - row_total)).astype(jnp.bfloat16)
    grad_queries = (
        jnp.einsum("ihlk,ikhe->ilhe", grad_scores, key_rows, preferred_element_type=jnp.float32)
        * score_scale
    )
    grad_keys = (
        jnp.einsum("ihlk,ilhe->ikhe", grad_scores, queries, preferred_element_type=jnp.float32)
        * score_scale
    )
    grad_queries = grad_queries.astype(jnp.bfloat16).reshape(images, latent_rows, local_width)
    grad_keys = grad_keys.astype(jnp.bfloat16).reshape(images, patches + latent_rows, local_width)
    grad_values = grad_values.astype(jnp.bfloat16).reshape(
        images, patches + latent_rows, local_width
    )
    media_grad_kv = jnp.concatenate([grad_keys[:, :patches], grad_values[:, :patches]], axis=2)
    latent_grad_qkv = jnp.concatenate(
        [grad_queries, grad_keys[:, patches:], grad_values[:, patches:]], axis=2
    )
    media_weight_grad = jnp.einsum(
        "ipd,ipe->de", media_normed, media_grad_kv, preferred_element_type=jnp.float32
    )
    latent_weight_grad = jnp.einsum(
        "ild,ile->de", latent_normed, latent_grad_qkv, preferred_element_type=jnp.float32
    )
    grad_wq = latent_weight_grad[:, :local_width]
    grad_wk = (
        media_weight_grad[:, :local_width] + latent_weight_grad[:, local_width : 2 * local_width]
    )
    grad_wv = media_weight_grad[:, local_width:] + latent_weight_grad[:, 2 * local_width :]
    grads_out = (
        lax.psum_scatter(grad_wq, "img", scatter_dimension=0, tiled=True),
        lax.psum_scatter(grad_wk, "img", scatter_dimension=0, tiled=True),
        lax.psum_scatter(grad_wv, "img", scatter_dimension=0, tiled=True),
        lax.psum_scatter(grad_wout, "img", scatter_dimension=0, tiled=True),
        lax.psum_scatter(grad_up, "img", scatter_dimension=0, tiled=True),
        lax.psum_scatter(grad_down, "img", scatter_dimension=0, tiled=True),
    )
    media_part = jnp.einsum(
        "ipe,de->ipd",
        media_grad_kv,
        joint_weight[:, local_width:],
        preferred_element_type=jnp.float32,
    )
    latent_part = jnp.einsum(
        "ile,de->ild", latent_grad_qkv, joint_weight, preferred_element_type=jnp.float32
    )
    media_share, latent_share = (
        lax.psum_scatter(
            media_part.astype(jnp.bfloat16), "head", scatter_dimension=1, tiled=True
        ).astype(jnp.float32),
        lax.psum_scatter(
            latent_part.astype(jnp.bfloat16), "head", scatter_dimension=1, tiled=True
        ).astype(jnp.float32),
    )
    media_rows = patches // groups
    media_puller = jax.vjp(
        layer_norm, rows_share(media_in, member, media_rows), norm_gains[0], norm_biases[0]
    )[1]
    grad_media_in, gain_media, bias_media = media_puller(media_share)
    latent_puller = jax.vjp(
        layer_norm, rows_share(latent_in, member, share_rows), norm_gains[1], norm_biases[1]
    )[1]
    grad_latent_norm, gain_latent, bias_latent = latent_puller(latent_share)
    latents_grad = (grad_residual_share + grad_latent_norm).astype(jnp.bfloat16)
    media_grad = grad_media_in.astype(jnp.bfloat16)
    gain_terms = jnp.stack([gain_media, gain_latent, gain_ffn])
    bias_terms = jnp.stack([bias_media, bias_latent, bias_ffn])
    gain_total, bias_total = (
        lax.psum_scatter(gain_terms, ("img", "head"), scatter_dimension=1, tiled=True),
        lax.psum_scatter(bias_terms, ("img", "head"), scatter_dimension=1, tiled=True),
    )
    return (
        latents_out,
        latents_grad,
        media_grad,
        grads_out[0],
        grads_out[1],
        grads_out[2],
        grads_out[3],
        grads_out[4],
        grads_out[5],
        gain_total,
        bias_total,
    )


def solution(mesh):
    return jax.shard_map(
        body,
        mesh=mesh,
        in_specs=(
            P("img", None, None),
            P("img", None, None),
            P("img"),
            P(None, "head"),
            P(None, "head"),
            P(None, "head"),
            P(None, "head"),
            P(None, "head"),
            P(None, "head"),
            P(),
            P(),
            P("img", None, None),
        ),
        out_specs=(
            P("img", None, None),
            P("img", "head", None),
            P("img", "head", None),
            P("img", "head"),
            P("img", "head"),
            P("img", "head"),
            P("img", "head"),
            P("img", "head"),
            P("img", "head"),
            P(None, ("img", "head")),
            P(None, ("img", "head")),
        ),
        check_vma=False,
    )
```

profile of v0, /device:TPU:0, one launch (start us, length us, event | category | flops | bytes accessed | tf_op | source)
XLA Modules:
  0.0 1304.9 jit_solution(8463983802196653508)
XLA Ops:
  10.2 2.9 multiply_reduce_fusion.3
  13.8 6.3 convert_reduce_fusion
  20.2 8.3 multiply_reduce_fusion
  32.9 8.5 fusion.23
  44.9 4.2 copy.55
  49.1 4.1 copy.56
  53.2 5.5 fusion.74
  58.7 4.1 convolution_convert_fusion.6
  62.8 2.7 convolution_convert_fusion.3
  65.9 123.6 %all-reduce.4.cloned.1.call-done = bf16[24,64,1024]{2,1,0:T(8,128)(2,1)} async-done(((bf16[24,64,1024]{2,1,0:T(8,128)(2,1)}), bf16[24,64,1024]{2,1,0:T(8,128)(2,1)}) %all-reduce.4.cloned.1.call-update) | async-done | bytes 3145744 | tf_op jit(solution)/shard_map/psum | solution.py:86
  189.5 3.9 fusion.18
  195.6 5.7 convert_reduce_fusion.4
  201.3 14.4 %multiply_convert_fusion = (bf16[24,64,1024]{2,1,0:T(8,128)(2,1)S(1)}, f32[24,64,1024]{2,1,0:T(8,128)S(1)}) fusion(f32[24,64,1024]{2,1,0:T(8,128)S(1)} %get-tuple-element.86, u32[64,1024]{1,0:T(8,128)S(1)} %get-tuple-element.55, u32[64,1024]{1,0:T(8,128)S(1)} %get-tuple-element.54), kind=kLoop, calls=%fused_computation.35 | loop fusion | flops 106954752 | bytes 16252928 | tf_op jit(solution)/shard_map/convert_element_type | solution.py:90
  215.7 6.4 add_convert_fusion.4
  222.0 6.7 convolution_convert_fusion.1
  228.8 4.8 convolution_convert_fusion.2
  233.7 222.0 %all-reduce.6.cloned.1.call-done = (bf16[24,64,1024]{2,1,0:T(8,128)(2,1)}, bf16[24,64,1024]{2,1,0:T(8,128)(2,1)}) async-done(((bf16[24,64,1024]{2,1,0:T(8,128)(2,1)}, bf16[24,64,1024]{2,1,0:T(8,128)(2,1)}), (bf16[24,64,1024]{2,1,0:T(8,128)(2,1)}, bf16[24,64,1024]{2,1,0:T(8,128)(2,1)})) %all-reduce.6.cloned.1.call-update) | async-done | bytes 6291472 | tf_op jit(solution)/shard_map/psum | solution.py:93
  455.7 5.4 convert_reduce_fusion.2
  461.1 6.5 fusion.10
  467.7 4.2 add_add_fusion.2
  471.9 2.6 copy-done.5
  475.9 3.3 convolution_convert_fusion.5
  489.1 4.7 convolution_convert_fusion.4
  495.6 2.7 slice.93
  502.0 8.5 convolution_convert_fusion
  510.6 8.4 convolution_bitcast_fusion
  519.0 5.2 convert_element_type.105
  524.3 14.3 %convert_element_type.106 = f32[24,256,1024]{2,1,0:T(8,128)} convert(bf16[24,256,1024]{2,1,0:T(8,128)(2,1)} %param.13) | non-fusion elementwise | flops 6291456 | bytes 37748736 | tf_op jit(solution)/shard_map/convert_element_type | solution.py:50
  540.1 3.2 dynamic-slice_reduce_fusion
  543.4 10.0 reduce-scatter.15.cloned.1.call-done
  555.6 2.5 fusion.36
  558.1 209.2 %reduce-scatter.17.cloned.1.call-done = bf16[24,64,1024]{2,1,0:T(8,128)(2,1)} async-done(((bf16[24,256,1024]{2,1,0:T(8,128)(2,1)}), bf16[24,64,1024]{2,1,0:T(8,128)(2,1)}) %reduce-scatter.17.cloned.1.call-update) | async-done | bytes 3145744 | tf_op jit(solution)/shard_map/reduce_scatter | solution.py:168
  767.3 6.1 multiply_reduce_fusion.1
  773.5 5.8 fusion.11
  781.9 10.5 convolution_bitcast_fusion.1
  792.5 6.3 fusion.47
  798.8 9.2 fusion.43
  808.1 4.1 fusion.42
  814.8 7.8 reduce-scatter.29.cloned.1.call-done
  824.7 3.3 add_convert_fusion.12
  828.1 6.1 add_convert_fusion.3
  834.2 126.4 %reduce-scatter.31.cloned.1.call-done = f32[32,3]{1,0:T(8,128)} async-done(((f32[1024,3]{1,0:T(8,128)}), f32[32,3]{1,0:T(8,128)}) %reduce-scatter.31.cloned.1.call-update) | async-done | bytes 400
  961.9 133.5 %reduce-scatter.33.cloned.1.call-done = f32[32,3]{1,0:T(8,128)} async-done(((f32[1024,3]{1,0:T(8,128)}), f32[32,3]{1,0:T(8,128)}) %reduce-scatter.33.cloned.1.call-update) | async-done | bytes 400
  1096.9 49.8 %reduce-scatter.27.cloned.1.call-done = f32[128,1024]{1,0:T(8,128)} async-done(((f32[1024,1024]{1,0:T(8,128)}), f32[128,1024]{1,0:T(8,128)}) %reduce-scatter.27.cloned.1.call-update) | async-done | bytes 524304 | tf_op jit(solution)/shard_map/reduce_scatter | solution.py:155
  1146.6 37.8 %reduce-scatter.25.cloned.1.call-done = f32[128,128]{1,0:T(8,128)} async-done(((f32[1024,128]{1,0:T(8,128)}), f32[128,128]{1,0:T(8,128)}) %reduce-scatter.25.cloned.1.call-update) | async-done | bytes 65552 | tf_op jit(solution)/shard_map/reduce_scatter | solution.py:154
  1184.5 37.7 %reduce-scatter.23.cloned.1.call-done = f32[128,128]{1,0:T(8,128)} async-done(((f32[1024,128]{1,0:T(8,128)}), f32[128,128]{1,0:T(8,128)}) %reduce-scatter.23.cloned.1.call-update) | async-done | bytes 65552 | tf_op jit(solution)/shard_map/reduce_scatter | solution.py:153
  1222.1 37.8 %reduce-scatter.21.cloned.1.call-done = f32[128,128]{1,0:T(8,128)} async-done(((f32[1024,128]{1,0:T(8,128)}), f32[128,128]{1,0:T(8,128)}) %reduce-scatter.21.cloned.1.call-update) | async-done | bytes 65552 | tf_op jit(solution)/shard_map/reduce_scatter | solution.py:152
  1259.9 37.7 %reduce-scatter.19.cloned.1.call-done = f32[128,128]{1,0:T(8,128)} async-done(((f32[1024,128]{1,0:T(8,128)}), f32[128,128]{1,0:T(8,128)}) %reduce-scatter.19.cloned.1.call-update) | async-done | bytes 65552 | tf_op jit(solution)/shard_map/reduce_scatter | solution.py:151
  (195 shorter events, 44.6 us)
Async XLA Ops:
  7.2 188.4 %copy-start = (bf16[1024,1024]{1,0:T(8,128)(2,1)S(1)}, bf16[1024,1024]{1,0:T(8,128)(2,1)}, u32[]{:S(2)}) copy-start(bf16[1024,1024]{1,0:T(8,128)(2,1)} %param.19) | copy-start | bytes 6291460
  7.2 182.3 %all-reduce.4.cloned.1.call-start = ((), (), s32[]{:S(2)}) async-start(), calls=%async_computation.10 | async-start | bytes 6291456 | tf_op jit(solution)/shard_map/psum | solution.py:86
  10.2 18.9 %copy-start.43 = (f32[24,64]{1,0:T(8,128)}, f32[24,64]{1,0:T(8,128)S(1)}, u32[]{:S(2)}) copy-start(f32[24,64]{1,0:T(8,128)S(1)} %broadcast_multiply_fusion.4) | copy-start | bytes 18436
  13.1 16.0 %copy-start.47 = (f32[24,64]{1,0:T(8,128)}, f32[24,64]{1,0:T(8,128)S(1)}, u32[]{:S(2)}) copy-start(f32[24,64]{1,0:T(8,128)S(1)} %add_rsqrt_fusion.1) | copy-start | bytes 18436
  13.2 15.9 %copy-start.41 = (f32[1,1024]{1,0:T(1,128)}, f32[1,1024]{1,0:T(1,128)S(1)}, u32[]{:S(2)}) copy-start(f32[1,1024]{1,0:T(1,128)S(1)} %get-tuple-element.76) | copy-start | bytes 12292
  13.2 454.5 %copy-start.39 = (f32[1,1024]{1,0:T(1,128)}, f32[1,1024]{1,0:T(1,128)S(1)}, u32[]{:S(2)}) copy-start(f32[1,1024]{1,0:T(1,128)S(1)} %get-tuple-element.74) | copy-start | bytes 12292
  13.8 15.3 %copy-start.50 = (f32[1,1024]{1,0:T(1,128)}, f32[1,1024]{1,0:T(1,128)S(1)}, u32[]{:S(2)}) copy-start(f32[1,1024]{1,0:T(1,128)S(1)} %get-tuple-element.79) | copy-start | bytes 12292
  20.1 8.4 copy-start.37
  20.1 9.0 copy-start.2
  20.1 9.0 copy-start.29
  20.1 9.0 copy-start.31
  20.2 9.0 copy-start.57
  32.9 20.3 %copy-start.17 = (bf16[24,64,128]{1,2,0:T(8,128)(2,1)}, bf16[24,64,128]{1,2,0:T(8,128)(2,1)S(1)}, u32[]{:S(2)}) copy-start(bf16[24,64,128]{1,2,0:T(8,128)(2,1)S(1)} %copy.81) | copy-start | bytes 1179652
  44.9 8.3 copy-start.54
  44.9 8.3 copy-start.55
  65.6 130.0 %copy-start.53 = (f32[1,1024]{1,0:T(1,128)S(1)}, f32[1,1024]{1,0:T(1,128)}, u32[]{:S(2)}) copy-start(f32[1,1024]{1,0:T(1,128)} %get-tuple-element.77) | copy-start | bytes 12292
  65.6 390.1 %all-reduce.6.cloned.1.call-start = ((), (), s32[]{:S(2)}) async-start(), calls=%async_computation.21 | async-start | bytes 12582912 | tf_op jit(solution)/shard_map/psum | solution.py:93
  201.2 14.4 %copy-start.14 = (bf16[24,64,1024]{2,1,0:T(8,128)(2,1)S(1)}, bf16[24,64,1024]{2,1,0:T(8,128)(2,1)}, u32[]{:S(2)}) copy-start(bf16[24,64,1024]{2,1,0:T(8,128)(2,1)} %param.23) | copy-start | bytes 9437188
  201.3 14.4 %copy-start.56 = (bf16[1024,1024]{1,0:T(8,128)(2,1)S(1)}, bf16[1024,1024]{1,0:T(8,128)(2,1)}, u32[]{:S(2)}) copy-start(bf16[1024,1024]{1,0:T(8,128)(2,1)} %param.20) | copy-start | bytes 6291460
  215.6 13.1 %copy-start.19 = (bf16[24,64,1024]{2,1,0:T(8,128)(2,1)}, bf16[24,64,1024]{2,1,0:T(8,128)(2,1)S(1)}, u32[]{:S(2)}) copy-start(bf16[24,64,1024]{2,1,0:T(8,128)(2,1)S(1)} %get-tuple-element.62) | copy-start | bytes 9437188
  233.6 319.7 %reduce-scatter.15.cloned.1.call-start = ((), (), s32[]{:S(2)}) async-start(), calls=%async_computation.11 | async-start | bytes 3932160 | tf_op jit(solution)/shard_map/reduce_scatter | solution.py:171
  455.7 12.0 copy-start.16
  461.1 6.6 copy-start.15
  467.7 6.8 copy-start.25
  493.9 273.5 %reduce-scatter.17.cloned.1.call-start = ((), (), s32[]{:S(2)}) async-start(), calls=%async_computation.12 | async-start | bytes 15728640 | tf_op jit(solution)/shard_map/reduce_scatter | solution.py:168
  493.9 8.0 copy-start.30
  493.9 8.0 copy-start.32
  501.9 8.5 copy-start.13
  510.5 312.2 %reduce-scatter.29.cloned.1.call-start = ((), (), s32[]{:S(2)}) async-start(), calls=%async_computation.18 | async-start | bytes 4718592 | tf_op jit(solution)/shard_map/reduce_scatter | solution.py:156
  519.0 441.6 %reduce-scatter.31.cloned.1.call-start = ((), (), s32[]{:S(2)}) async-start(), calls=%async_computation.19 | async-start | bytes 540672
  538.6 14.7 %copy-start.42 = (f32[1,1024]{1,0:T(1,128)S(1)}, f32[1,1024]{1,0:T(1,128)}, u32[]{:S(2)}) copy-start(f32[1,1024]{1,0:T(1,128)} %copy-done.41) | copy-start | bytes 12292
  773.4 8.5 copy-start.40
  773.4 18.9 %copy-start.33 = (f32[24,64]{1,0:T(8,128)}, f32[24,64]{1,0:T(8,128)S(1)}, u32[]{:S(2)}) copy-start(f32[24,64]{1,0:T(8,128)S(1)} %get-tuple-element.80) | copy-start | bytes 18436
  773.4 18.9 %copy-start.35 = (f32[24,64]{1,0:T(8,128)}, f32[24,64]{1,0:T(8,128)S(1)}, u32[]{:S(2)}) copy-start(f32[24,64]{1,0:T(8,128)S(1)} %get-tuple-element.81) | copy-start | bytes 18436
  780.4 315.1 %reduce-scatter.33.cloned.1.call-start = ((), (), s32[]{:S(2)}) async-start(), calls=%async_computation.20 | async-start | bytes 540672
  781.6 365.1 %reduce-scatter.27.cloned.1.call-start = ((), (), s32[]{:S(2)}) async-start(), calls=%async_computation.17 | async-start | bytes 4718592 | tf_op jit(solution)/shard_map/reduce_scatter | solution.py:155
  792.4 392.0 %reduce-scatter.25.cloned.1.call-start = ((), (), s32[]{:S(2)}) async-start(), calls=%async_computation.16 | async-start | bytes 589824 | tf_op jit(solution)/shard_map/reduce_scatter | solution.py:154
  798.8 9.3 copy-start.27
  798.8 9.3 copy-start.44
  798.8 9.3 copy-start.51
  808.1 414.1 %reduce-scatter.23.cloned.1.call-start = ((), (), s32[]{:S(2)}) async-start(), calls=%async_computation.15 | async-start | bytes 589824 | tf_op jit(solution)/shard_map/reduce_scatter | solution.py:153
  812.2 12.5 copy-start.11
  812.2 15.8 %copy-start.45 = (f32[24,64]{1,0:T(8,128)S(1)}, f32[24,64]{1,0:T(8,128)}, u32[]{:S(2)}) copy-start(f32[24,64]{1,0:T(8,128)} %get-tuple-element.45) | copy-start | bytes 18436
  812.2 15.8 %copy-start.34 = (f32[24,64]{1,0:T(8,128)S(1)}, f32[24,64]{1,0:T(8,128)}, u32[]{:S(2)}) copy-start(f32[24,64]{1,0:T(8,128)} %copy-done.33) | copy-start | bytes 18436
  812.2 15.8 %copy-start.36 = (f32[24,64]{1,0:T(8,128)S(1)}, f32[24,64]{1,0:T(8,128)}, u32[]{:S(2)}) copy-start(f32[24,64]{1,0:T(8,128)} %copy-done.35) | copy-start | bytes 18436
  813.5 446.4 %reduce-scatter.21.cloned.1.call-start = ((), (), s32[]{:S(2)}) async-start(), calls=%async_computation.14 | async-start | bytes 589824 | tf_op jit(solution)/shard_map/reduce_scatter | solution.py:152
  814.2 483.4 %reduce-scatter.19.cloned.1.call-start = ((), (), s32[]{:S(2)}) async-start(), calls=%async_computation.13 | async-start | bytes 589824 | tf_op jit(solution)/shard_map/reduce_scatter | solution.py:151
  828.0 469.6 %copy-start.1 = (bf16[1024,1024]{1,0:T(8,128)(2,1)S(1)}, bf16[1024,1024]{1,0:T(8,128)(2,1)}, u32[]{:S(2)}) copy-start(bf16[1024,1024]{1,0:T(8,128)(2,1)} %param.19) | copy-start | bytes 6291460
  (24 other events, 114.2 us)
Sparse Core Ops, SparseCore 0:
  65.7 123.7 all-reduce.3
  233.7 221.8 all-reduce.5
  494.0 59.2 reduce-scatter.14
  555.5 211.7 reduce-scatter.16
  770.5 52.0 reduce-scatter.28
  824.8 135.7 reduce-scatter.30
  962.8 132.6 reduce-scatter.32
  1099.4 47.1 reduce-scatter.26
  1150.3 34.1 reduce-scatter.24
  1188.0 34.1 reduce-scatter.22
  1225.8 34.1 reduce-scatter.20
  1263.5 34.1 reduce-scatter.18
where the time goes:
time: 1310 us; the launch traced here: 1300 us
  waiting for transfers between devices  1030 us (79%)
  other arithmetic  112 us (9%)
  matrix products  107 us (8%)
  local copies, waits for them, and re-layouts  34.5 us (3%)
  between operations  15.6 us (1%)
    unnamed x14, waiting for transfers between devices  261 us
    psum x1, waiting for transfers between devices, body(): lax.psum(mlp_part.astype(jnp.bfloat16), 'head').astype(jnp.float32)  222 us
    reduce_scatter x1, waiting for transfers between devices, body(): lax.psum_scatter(media_part.astype(jnp.bfloat16), 'head', scatter_dimensi...  209 us
    psum x1, waiting for transfers between devices, body(): lax.psum(attn_part.astype(jnp.bfloat16), 'head').astype(jnp.float32)  124 us
    reduce_scatter x1, waiting for transfers between devices, body(): lax.psum_scatter(grad_up, 'img', scatter_dimension=0, tiled=True)  49.8 us
    reduce_scatter x1, waiting for transfers between devices, body(): lax.psum_scatter(grad_wout, 'img', scatter_dimension=0, tiled=True)  37.8 us
    reduce_scatter x1, waiting for transfers between devices, body(): lax.psum_scatter(grad_wk, 'img', scatter_dimension=0, tiled=True)  37.8 us
    reduce_scatter x1, waiting for transfers between devices, body(): lax.psum_scatter(grad_wq, 'img', scatter_dimension=0, tiled=True)  37.7 us
  transfers between devices with their start and end apart: 12, of which 12 were waited for; matrix products, arithmetic and copies ran while one was open for 9% of the time, Pallas kernels for 0%

commit v1 on v0

v1 whole, which is shorter than its diff:
```python
import jax
import jax.numpy as jnp
from jax import lax
from jax.sharding import PartitionSpec as P

HEAD_DIM = 64
epsilon = 1e-05
BF = jnp.bfloat16
F32 = jnp.float32


def layer_stats(values):
    center = jnp.mean(values, axis=-1, keepdims=True)
    centered = values - center
    spread = jnp.mean(centered * centered, axis=-1, keepdims=True)
    scale = lax.rsqrt(spread + epsilon)
    return centered * scale, scale


def layer_back(grad, gain_row, xhat, scale):
    weighted = grad * gain_row
    first = jnp.mean(weighted, axis=-1, keepdims=True)
    second = jnp.mean(weighted * xhat, axis=-1, keepdims=True)
    return (weighted - first - xhat * second) * scale


def exchange(values, axis, bit):
    count = lax.axis_size(axis)
    return lax.ppermute(values, axis, [(place, place ^ bit) for place in range(count)])


def ordered_pair(bit, mine, other, dim):
    low = jnp.where(bit == 0, mine, other)
    high = jnp.where(bit == 0, other, mine)
    return jnp.concatenate([low, high], axis=dim)


def bit_count(count):
    return count.bit_length() - 1


def gather_img(piece, order):
    bits = len(order)
    place = lax.axis_index("img")
    held = piece.reshape((1,) * bits + piece.shape)
    for bit in order:
        other = exchange(held, "img", 1 << bit)
        held = ordered_pair((place >> bit) & 1, held, other, bits - 1 - bit)
    return held.reshape((-1,) + piece.shape[1:])


def scatter_img(values, order, dim, last):
    bits = len(order)
    place = lax.axis_index("img")
    shape = values.shape
    held = values.reshape(shape[:dim] + (2,) * bits + (-1,) + shape[dim + 1 :])
    for step, bit in enumerate(order):
        mine = (place >> bit) & 1
        axis = dim + bits - 1 - bit
        keep = lax.dynamic_slice_in_dim(held, mine, 1, axis)
        send = lax.dynamic_slice_in_dim(held, 1 - mine, 1, axis)
        got = exchange(send, "img", 1 << bit)
        held = keep.astype(F32) + got.astype(F32)
        if step < bits - 1 or not last:
            held = held.astype(BF)
    return held.reshape(shape[:dim] + (-1,) + shape[dim + 1 :])


def by_source(pieces):
    member = lax.axis_index("head")
    level = [piece[None] for piece in pieces]
    bit = 0
    while len(level) > 1:
        level = [
            ordered_pair((member >> bit) & 1, level[at], level[at + 1], 0)
            for at in range(0, len(level), 2)
        ]
        bit += 1
    return level[0]


def body(
    latents,
    media,
    valid_counts,
    w_query,
    w_key,
    w_value,
    w_out,
    w_up,
    w_down,
    norm_gains,
    norm_biases,
    cotangent,
):
    groups = lax.axis_size("head")
    count = lax.axis_size("img")
    member = lax.axis_index("head")
    place = lax.axis_index("img")
    bits = bit_count(count)
    order_a = list(range(bits))
    order_b = [0] + list(range(bits - 1, 0, -1))
    gather_a = order_a[:0:-1] + [0]
    gather_b = order_b[:0:-1] + [0]
    total_images, patches, width = media.shape
    rows = latents.shape[1]
    images = total_images // groups
    local = w_query.shape[1]
    hidden_local = w_up.shape[1]
    scale = HEAD_DIM ** (-0.5)
    part = width // count

    def mine(values):
        return lax.dynamic_slice_in_dim(values, member * images, images, 0)

    attn_pack = jnp.concatenate([w_query, w_key, w_value, w_out], axis=1)
    attn_piece = lax.dynamic_slice_in_dim(attn_pack, place * part, part, 0)
    attn_got = jnp.concatenate([exchange(attn_piece, "head", j) for j in range(1, groups)], axis=1)
    half = attn_got.shape[1] // 2
    attn_all = jnp.concatenate(
        [attn_pack, gather_img(attn_got[:, :half], gather_a), gather_img(attn_got[:, half:], gather_b)],
        axis=1,
    ).reshape(width, groups, 4, local)
    up_piece = lax.dynamic_slice_in_dim(w_up, place * part, part, 0)
    down_piece = lax.dynamic_slice_in_dim(w_down, place * part, part, 0)
    ups, downs = [w_up], [w_down]
    for j in range(1, groups):
        ups.append(gather_img(exchange(up_piece, "head", j), gather_a))
        downs.append(gather_img(exchange(down_piece, "head", j), gather_b))

    latent_in = mine(latents).astype(F32)
    media_in = mine(media).astype(F32)
    upstream = mine(cotangent)
    counts = mine(valid_counts)
    media_hat, media_scale = layer_stats(media_in)
    latent_hat, latent_scale = layer_stats(latent_in)
    media_normed = (media_hat * norm_gains[0] + norm_biases[0]).astype(BF)
    latent_normed = (latent_hat * norm_gains[1] + norm_biases[1]).astype(BF)
    wide = groups * local
    wq, wk, wv, wo = (attn_all[:, :, at].reshape(width, wide) for at in range(4))
    w_kv = jnp.concatenate([wk, wv], axis=1)
    w_qkv = jnp.concatenate([wq, wk, wv], axis=1)

    def mm(a, b, dims):
        return lax.dot_general(a, b, (dims, ((), ())), preferred_element_type=F32)

    kv_media = mm(media_normed.reshape(-1, width), w_kv, ((1,), (0,))).astype(BF)
    qkv_lat = mm(latent_normed.reshape(-1, width), w_qkv, ((1,), (0,))).astype(BF)
    kv_media = kv_media.reshape(images, patches, 2 * wide)
    qkv_lat = qkv_lat.reshape(images, rows, 3 * wide)
    heads = wide // HEAD_DIM
    queries = qkv_lat[..., :wide].reshape(images, rows, heads, HEAD_DIM)
    kv = jnp.concatenate([kv_media, qkv_lat[..., wide:]], axis=1)
    key_rows = kv[..., :wide].reshape(images, patches + rows, heads, HEAD_DIM)
    value_rows = kv[..., wide:].reshape(images, patches + rows, heads, HEAD_DIM)
    positions = lax.iota(jnp.int32, patches + rows)
    allowed = (positions[None, :] < counts[:, None]) | (positions[None, :] >= patches)
    scores = jnp.einsum("ilhe,ikhe->ihlk", queries, key_rows, preferred_element_type=F32) * scale
    scores = jnp.where(allowed[:, None, None, :], scores, -1e30)
    attention = jax.nn.softmax(scores, axis=-1)
    attention_low = attention.astype(BF)
    attended = jnp.einsum("ihlk,ikhe->ilhe", attention_low, value_rows, preferred_element_type=F32)
    attended = attended.astype(BF).reshape(images * rows, wide)
    residual = latent_in.reshape(-1, width) + mm(attended, wo, ((1,), (1,)))
    res_hat, res_scale = layer_stats(residual)
    ffn_low = (res_hat * norm_gains[2] + norm_biases[2]).astype(BF)
    cot = upstream.reshape(-1, width)
    mlp = jnp.zeros(residual.shape, F32)
    grad_ffn = jnp.zeros(residual.shape, F32)
    ffn_grads = []
    for j in range(groups):
        pre = mm(ffn_low, ups[j], ((1,), (0,)))
        phi = 0.5 * (1.0 + lax.erf(pre * (0.5**0.5)))
        density = jnp.exp(-0.5 * pre * pre) * 0.3989422804014327
        hidden = (pre * phi).astype(BF)
        grad_pre = (mm(cot, downs[j], ((1,), (0,))) * (phi + pre * density)).astype(BF)
        mlp = mlp + mm(hidden, downs[j], ((1,), (1,)))
        grad_ffn = grad_ffn + mm(grad_pre, ups[j], ((1,), (1,)))
        up_grad = mm(ffn_low, grad_pre, ((0,), (0,))).astype(BF)
        down_grad = mm(cot, hidden, ((0,), (0,))).astype(BF)
        ffn_grads.append(
            (scatter_img(up_grad, order_a, 0, j == 0), scatter_img(down_grad, order_b, 0, j == 0))
        )
    out_mine = (residual + mlp).astype(BF).reshape(images, rows, width)
    latents_out = by_source(
        [out_mine] + [exchange(out_mine, "head", j) for j in range(1, groups)]
    ).reshape(total_images, rows, width)
    up_total = ffn_grads[0][0].astype(F32)
    down_total = ffn_grads[0][1].astype(F32)
    for j in range(1, groups):
        up_total = up_total + exchange(ffn_grads[j][0].astype(BF), "head", j).astype(F32)
        down_total = down_total + exchange(ffn_grads[j][1].astype(BF), "head", j).astype(F32)

    grad_residual = cot.astype(F32) + layer_back(grad_ffn, norm_gains[2], res_hat, res_scale)
    gain_ffn = jnp.sum(grad_ffn * res_hat, axis=0)
    bias_ffn = jnp.sum(grad_ffn, axis=0)
    grad_low = grad_residual.astype(BF)
    grad_wo = mm(grad_low, attended, ((0,), (0,)))
    grad_attended = mm(grad_low, wo, ((1,), (0,))).astype(BF).reshape(images, rows, heads, HEAD_DIM)
    grad_values = jnp.einsum(
        "ihlk,ilhe->ikhe", attention_low, grad_attended, preferred_element_type=F32
    )
    grad_attention = jnp.einsum(
        "ilhe,ikhe->ihlk", grad_attended, value_rows, preferred_element_type=F32
    )
    row_total = jnp.sum(attention * grad_attention, axis=-1, keepdims=True)
    grad_scores = (attention * (grad_attention - row_total)).astype(BF)
    grad_q = (
        jnp.einsum("ihlk,ikhe->ilhe", grad_scores, key_rows, preferred_element_type=F32) * scale
    )
    grad_k = jnp.einsum("ihlk,ilhe->ikhe", grad_scores, queries, preferred_element_type=F32) * scale
    grad_q = grad_q.astype(BF).reshape(images, rows, wide)
    grad_kv = jnp.concatenate(
        [
            grad_k.astype(BF).reshape(images, patches + rows, wide),
            grad_values.astype(BF).reshape(images, patches + rows, wide),
        ],
        axis=2,
    )
    media_gkv = grad_kv[:, :patches].reshape(-1, 2 * wide)
    latent_g = jnp.concatenate([grad_q, grad_kv[:, patches:]], axis=2).reshape(-1, 3 * wide)
    media_g = mm(media_gkv, w_kv, ((1,), (1,))).reshape(images, patches, width)
    latent_gn = mm(latent_g, w_qkv, ((1,), (1,))).reshape(images, rows, width)
    media_grad = layer_back(media_g, norm_gains[0], media_hat, media_scale).astype(BF)
    latents_grad = (
        grad_residual.reshape(images, rows, width)
        + layer_back(latent_gn, norm_gains[1], latent_hat, latent_scale)
    ).astype(BF)

    def spread(values):
        split = values.reshape(images, groups, -1, width)
        pieces = []
        for j in range(groups):
            piece = lax.dynamic_index_in_dim(split, member ^ j, 1, keepdims=False)
            pieces.append(piece if j == 0 else exchange(piece, "head", j))
        stacked = by_source(pieces)
        return stacked.reshape(total_images, -1, width)

    media_out = spread(media_grad)
    latents_back = spread(latents_grad)
    kv_wgrad = mm(media_normed.reshape(-1, width), media_gkv, ((0,), (0,)))
    qkv_wgrad = mm(latent_normed.reshape(-1, width), latent_g, ((0,), (0,)))
    all_wgrad = jnp.concatenate(
        [qkv_wgrad[:, :wide], qkv_wgrad[:, wide:] + kv_wgrad, grad_wo], axis=1
    ).astype(BF)
    all_wgrad = all_wgrad.reshape(width, 4, groups, local)
    attn_a = scatter_img(all_wgrad[:, :2], order_a, 0, False)
    attn_b = scatter_img(all_wgrad[:, 2:], order_b, 0, False)
    attn_sum = jnp.concatenate([attn_a, attn_b], axis=1)
    attn_total = attn_sum[:, :, 0].astype(F32)
    for j in range(1, groups):
        attn_total = attn_total + exchange(attn_sum[:, :, j], "head", j).astype(F32)

    norm_terms = jnp.stack(
        [
            jnp.sum(media_g * media_hat, axis=(0, 1)),
            jnp.sum(latent_gn * latent_hat, axis=(0, 1)),
            gain_ffn,
            jnp.sum(media_g, axis=(0, 1)),
            jnp.sum(latent_gn, axis=(0, 1)),
            bias_ffn,
        ]
    )
    for bit in range(bits):
        norm_terms = norm_terms + exchange(norm_terms, "img", 1 << bit)
    for bit in range(bit_count(groups)):
        norm_terms = norm_terms + exchange(norm_terms, "head", 1 << bit)
    share = width // (count * groups)
    norm_mine = lax.dynamic_slice_in_dim(norm_terms, (place * groups + member) * share, share, 1)
    return (
        latents_out,
        latents_back,
        media_out,
        attn_total[:, 0],
        attn_total[:, 1],
        attn_total[:, 2],
        attn_total[:, 3],
        up_total,
        down_total,
        norm_mine[:3],
        norm_mine[3:],
    )


def solution(mesh):
    return jax.shard_map(
        body,
        mesh=mesh,
        in_specs=(
            P("img", None, None),
            P("img", None, None),
            P("img"),
            P(None, "head"),
            P(None, "head"),
            P(None, "head"),
            P(None, "head"),
            P(None, "head"),
            P(None, "head"),
            P(),
            P(),
            P("img", None, None),
        ),
        out_specs=(
            P("img", None, None),
            P("img", "head", None),
            P("img", "head", None),
            P("img", "head"),
            P("img", "head"),
            P("img", "head"),
            P("img", "head"),
            P("img", "head"),
            P("img", "head"),
            P(None, ("img", "head")),
            P(None, ("img", "head")),
        ),
        check_vma=False,
    )
```

time: 1310 us -> 671 us (0.51)
  waiting for transfers between devices: 1030 us -> 282 us
  starting transfers between devices: 1 us -> 118 us
  local copies, waits for them, and re-layouts: 34.5 us -> 95.3 us
  other arithmetic: 112 us -> 68.7 us
    reduce_scatter x8 -> x0, waiting for transfers between devices: 428 us -> none  [the longest x1 209 us: body(): lax.psum_scatter(media_part.astype(jnp.bfloat16), 'head', scatter_dimensi...]
    psum x2 -> x0, waiting for transfers between devices: 346 us -> none  [the longest x1 222 us: body(): lax.psum(mlp_part.astype(jnp.bfloat16), 'head').astype(jnp.float32)]
    ppermute x0 -> x86, waiting for transfers between devices: none -> 282 us  [exchange(): lax.ppermute(values, axis, [(place, place ^ bit) for place in range(count)])]
    unnamed x14 -> x0, waiting for transfers between devices: 261 us -> none
    ppermute x0 -> x86, starting transfers between devices: none -> 118 us  [exchange(): lax.ppermute(values, axis, [(place, place ^ bit) for place in range(count)])]
    reduce_sum x14 -> x5, other arithmetic: 58.4 us -> 7.17 us  [the longest x2 3.67 us: layer_stats(): center = jnp.mean(values, axis=-1, keepdims=True)]
    convert_element_type x6 -> x26, other arithmetic: 44.4 us -> 21.4 us  [the longest x20 8.45 us: scatter_img(): held = held.astype(BF)]
    concatenate x1 -> x31, other arithmetic: 2.25 us -> 21.8 us  [the longest x27 14.9 us: ordered_pair(): return jnp.concatenate([low, high], axis=dim)]
  transfers between devices with their start and end apart: 12 -> 86, of which waited for: 12 -> 31; matrix products, arithmetic and copies ran while one was open for 9% -> 36% of each run, Pallas kernels for 0% -> 0%
where the time goes in v1:
time: 671 us; the launch traced here: 664 us
  waiting for transfers between devices  282 us (42%)
  starting transfers between devices  118 us (18%)
  matrix products  95.7 us (14%)
  local copies, waits for them, and re-layouts  95.3 us (14%)
  other arithmetic  68.7 us (10%)
    ppermute x86, waiting for transfers between devices, exchange(): lax.ppermute(values, axis, [(place, place ^ bit) for place in range(count)])  282 us
    ppermute x86, starting transfers between devices, exchange(): lax.ppermute(values, axis, [(place, place ^ bit) for place in range(count)])  118 us
    dot_general x33, matrix products, mm(): return lax.dot_general(a, b, (dims, ((), ())), preferred_element_type=F32)  76.9 us
    unnamed x274, local copies, waits for them, and re-layouts  32.4 us
    concatenate x27, other arithmetic, ordered_pair(): return jnp.concatenate([low, high], axis=dim)  14.9 us
  transfers between devices with their start and end apart: 86, of which 31 were waited for; matrix products, arithmetic and copies ran while one was open for 36% of the time, Pallas kernels for 0%

profile of v1, /device:TPU:0, one launch (start us, length us, event | category | flops | bytes accessed | tf_op | source)
XLA Modules:
  0.0 663.9 jit_solution(1187660291054255249)
XLA Ops:
  1.7 3.1 collective-permute-start
  10.0 3.5 collective-permute-start.17
  32.5 4.0 fusion.8
  47.9 3.7 collective-permute-start.25
  55.4 9.3 %collective-permute-done.21 = bf16[128,1024]{1,0:T(8,128)(2,1)S(1)} collective-permute-done((bf16[128,1024]{1,0:T(8,128)(2,1)}, bf16[128,1024]{1,0:T(8,128)(2,1)S(1)}, u32[]{:S(2)}, u32[]{:S(2)}) %collective-permute-start.21) | collective-permute-done | bytes 262176 | tf_op jit(solution)/shard_map/ppermute | solution.py:29
  83.3 4.9 collective-permute-done.7
  92.6 8.2 %collective-permute-done.11 = bf16[2,1,1,128,1024]{4,3,2,1,0:T(8,128)(2,1)S(1)} collective-permute-done((bf16[2,1,1,128,1024]{4,3,2,1,0:T(8,128)(2,1)S(1)}, bf16[2,1,1,128,1024]{4,3,2,1,0:T(8,128)(2,1)S(1)}, u32[]{:S(2)}, u32[]{:S(2)}) %collective-permute-start.11) | collective-permute-done | bytes 524320 | tf_op jit(solution)/shard_map/ppermute | solution.py:29
  103.9 5.0 collective-permute-done.19
  126.6 3.8 fusion.97
  134.3 3.6 convolution_convert_fusion.1
  139.5 3.8 convolution_convert_fusion
  148.8 5.0 copy.43
  153.8 3.7 fusion.101
  157.5 4.1 fusion.49
  212.5 4.8 multiply_reduce_fusion.1
  217.3 3.1 multiply_convert_fusion.1
  239.4 4.1 copy.50
  243.5 4.1 copy.51
  247.7 10.0 %fusion.13 = (f32[1024]{0:T(1024)}, f32[6,256]{1,0:T(8,128)}, f32[6,256]{1,0:T(8,128)}, f32[1024]{0:T(1024)}, f32[6,256,1024]{2,1,0:T(8,128)}) fusion(f32[6,256]{1,0:T(8,128)S(1)} %add_rsqrt_fusion, f32[6,256]{1,0:T(8,128)S(1)} %broadcast_multiply_fusion.2, bf16[24,256,1024]{2,1,0:T(8,128)(2,1)} %param.13, s32[]{:T(128)S(6)} %select_n.462, ...), kind=kOutput, calls=%fused_computation.15 | convolution fusion | flops 3247434752 | bytes 15503364 | tf_op jit(solution)/shard_map/dot_general | solution.py:145
  259.8 3.3 multiply_reduce_fusion.3
  265.1 6.9 %fusion.15 = bf16[1024,1024]{1,0:T(8,128)(2,1)} fusion(f32[1024,1536]{1,0:T(8,128)S(1)} %convolution_bitcast_fusion, bf16[6,256,1024]{2,1,0:T(8,128)(2,1)S(1)} %copy-done.44, bf16[6,320,512]{2,1,0:T(8,128)(2,1)S(1)} %copy-done.12, bf16[6,320,512]{2,1,0:T(8,128)(2,1)S(1)} %copy-done.11), kind=kOutput, calls=%fused_computation.25 | convolution fusion | flops 3229614080 | bytes 13369344 | tf_op jit(solution)/shard_map/dot_general | solution.py:145
  289.4 3.6 pad_maximum_fusion
  293.0 7.7 %convert_element_type.450 = bf16[1024,4,4,128]{3,2,1,0:T(4,128)(2,1)} reshape(bf16[1024,2048]{1,0:T(8,128)(2,1)} %pad_maximum_fusion) | data formatting | bytes 8388608 | tf_op jit(solution)/shard_map/convert_element_type | solution.py:245
  300.7 3.1 fusion.96
  309.3 3.7 fusion.12
  324.3 11.1 %collective-permute-start.84 = (f32[6,1024]{1,0:T(8,128)S(1)}, f32[6,1024]{1,0:T(8,128)S(1)}, u32[]{:S(2)}, u32[]{:S(2)}) collective-permute-start(f32[6,1024]{1,0:T(8,128)S(1)} %add.449), channel_id=1, source_target_pairs={{0,1},{1,0},{2,3},{3,2},{4,5},{5,4},{6,7},{7,6},{8,9},{9,8},{10,11... | collective-permute-start | bytes 73736 | tf_op jit(solution)/shard_map/ppermute | solution.py:29
  337.4 3.3 collective-permute-start.85
  340.8 31.1 %collective-permute-done.85 = f32[6,1024]{1,0:T(8,128)S(1)} collective-permute-done((f32[6,1024]{1,0:T(8,128)S(1)}, f32[6,1024]{1,0:T(8,128)S(1)}, u32[]{:S(2)}, u32[]{:S(2)}) %collective-permute-start.85) | collective-permute-done | bytes 24608 | tf_op jit(solution)/shard_map/ppermute | solution.py:29
  374.9 12.6 %collective-permute-done.37 = bf16[6,16,1024]{2,1,0:T(8,128)(2,1)S(1)} collective-permute-done((bf16[6,16,1024]{2,1,0:T(8,128)(2,1)S(1)}, bf16[6,16,1024]{2,1,0:T(8,128)(2,1)S(1)}, u32[]{:S(2)}, u32[]{:S(2)}) %collective-permute-start.37) | collective-permute-done | bytes 196640 | tf_op jit(solution)/shard_map/ppermute | solution.py:29
  389.0 3.3 collective-permute-start.33
  398.9 60.5 %collective-permute-done.39 = bf16[6,64,1024]{2,1,0:T(8,128)(2,1)S(1)} collective-permute-done((bf16[6,64,1024]{2,1,0:T(8,128)(2,1)S(1)}, bf16[6,64,1024]{2,1,0:T(8,128)(2,1)S(1)}, u32[]{:S(2)}, u32[]{:S(2)}) %collective-permute-start.39) | collective-permute-done | bytes 786464 | tf_op jit(solution)/shard_map/ppermute | solution.py:29
  463.9 16.9 %collective-permute-done.41 = bf16[6,64,1024]{2,1,0:T(8,128)(2,1)S(1)} collective-permute-done((bf16[6,64,1024]{2,1,0:T(8,128)(2,1)S(1)}, bf16[6,64,1024]{2,1,0:T(8,128)(2,1)S(1)}, u32[]{:S(2)}, u32[]{:S(2)}) %collective-permute-start.41) | collective-permute-done | bytes 786464 | tf_op jit(solution)/shard_map/ppermute | solution.py:29
  487.1 6.6 collective-permute-done.52
  505.5 14.2 %collective-permute-done.70 = bf16[1,2,1,128,1024]{4,3,2,1,0:T(8,128)(2,1)S(1)} collective-permute-done((bf16[1,2,1,128,1024]{4,3,2,1,0:T(8,128)(2,1)S(1)}, bf16[1,2,1,128,1024]{4,3,2,1,0:T(8,128)(2,1)S(1)}, u32[]{:S(2)}, u32[]{:S(2)}) %collective-permute-start.70) | collective-permute-done | bytes 524320 | tf_op jit(solution)/shard_map/ppermute | solution.py:29
  520.5 10.5 %collective-permute-done.74 = bf16[1,2,1,128,1024]{4,3,2,1,0:T(8,128)(2,1)S(1)} collective-permute-done((bf16[1,2,1,128,1024]{4,3,2,1,0:T(8,128)(2,1)S(1)}, bf16[1,2,1,128,1024]{4,3,2,1,0:T(8,128)(2,1)S(1)}, u32[]{:S(2)}, u32[]{:S(2)}) %collective-permute-start.74) | collective-permute-done | bytes 524320 | tf_op jit(solution)/shard_map/ppermute | solution.py:29
  531.7 9.4 %collective-permute-done.78 = bf16[1,2,1,128,1024]{4,3,2,1,0:T(8,128)(2,1)S(1)} collective-permute-done((bf16[1,2,1,128,1024]{4,3,2,1,0:T(8,128)(2,1)S(1)}, bf16[1,2,1,128,1024]{4,3,2,1,0:T(8,128)(2,1)S(1)}, u32[]{:S(2)}, u32[]{:S(2)}) %collective-permute-start.78) | collective-permute-done | bytes 524320 | tf_op jit(solution)/shard_map/ppermute | solution.py:29
  544.6 11.2 %collective-permute-done.63 = bf16[2,1,1,128,1024]{4,3,2,1,0:T(8,128)(2,1)S(1)} collective-permute-done((bf16[2,1,1,128,1024]{4,3,2,1,0:T(8,128)(2,1)S(1)}, bf16[2,1,1,128,1024]{4,3,2,1,0:T(8,128)(2,1)S(1)}, u32[]{:S(2)}, u32[]{:S(2)}) %collective-permute-start.63) | collective-permute-done | bytes 524320 | tf_op jit(solution)/shard_map/ppermute | solution.py:29
  558.3 8.8 %collective-permute-done.43 = bf16[2,1,1,128,2,4,128]{6,3,2,1,0,5,4:T(8,128)(2,1)S(1)} collective-permute-done((bf16[2,1,1,128,2,4,128]{6,3,2,1,0,5,4:T(8,128)(2,1)S(1)}, bf16[2,1,1,128,2,4,128]{6,3,2,1,0,5,4:T(8,128)(2,1)S(1)}, u32[]{:S(2)}, u32[]{:S(2)}) %collective-permute-start.43) | collective-permute-done | bytes 524320 | tf_op jit(solution)/shard_map/ppermute | solution.py:29
  567.9 4.8 collective-permute-done.71
  573.4 4.9 collective-permute-done.75
  578.9 5.0 collective-permute-done.79
  584.6 3.0 collective-permute-done.47
  588.2 4.1 collective-permute-done.44
  593.1 14.6 %collective-permute-start.48 = (bf16[128,4,128]{2,0,1:T(8,128)(2,1)S(1)}, bf16[128,4,128]{2,0,1:T(8,128)(2,1)S(1)}, u32[]{:S(2)}, u32[]{:S(2)}) collective-permute-start(bf16[128,4,128]{2,0,1:T(8,128)(2,1)S(1)} %get-tuple-element.89), channel_id=1, source_target_pairs={{0,1},{1,0},{2,3},{3,2},{4,5},{5,4},{6,7},{7,6},{8,9},{9,8},{10,11... | collective-permute-start | bytes 393224 | tf_op jit(solution)/shard_map/ppermute | solution.py:29
  607.8 4.7 collective-permute-start.49
  627.2 13.0 %collective-permute-done.76 = bf16[128,1024]{1,0:T(8,128)(2,1)S(1)} collective-permute-done((bf16[128,1024]{1,0:T(8,128)(2,1)S(1)}, bf16[128,1024]{1,0:T(8,128)(2,1)S(1)}, u32[]{:S(2)}, u32[]{:S(2)}) %collective-permute-start.76) | collective-permute-done | bytes 262176 | tf_op jit(solution)/shard_map/ppermute | solution.py:29
  640.2 3.0 collective-permute-start.65
  644.2 18.4 %collective-permute-done.61 = bf16[128,1024]{1,0:T(8,128)(2,1)S(1)} collective-permute-done((bf16[128,1024]{1,0:T(8,128)(2,1)S(1)}, bf16[128,1024]{1,0:T(8,128)(2,1)S(1)}, u32[]{:S(2)}, u32[]{:S(2)}) %collective-permute-start.61) | collective-permute-done | bytes 262176 | tf_op jit(solution)/shard_map/ppermute | solution.py:29
  (628 shorter events, 265.3 us)
Async XLA Ops:
  1.7 37.1 %collective-permute-start = (bf16[128,512]{1,0:T(8,128)(2,1)S(1)}, bf16[128,512]{1,0:T(8,128)(2,1)}, u32[]{:S(2)}, u32[]{:S(2)}) collective-permute-start(bf16[128,512]{1,0:T(8,128)(2,1)S(1)} %fusion.79), channel_id=1, source_target_pairs={{0,1},{1,0},{2,3},{3,2},{4,5},{5,4},{6,7},{7,6},{8,9},{9,8},{10,11... | collective-permute-start | bytes 393224 | tf_op jit(solution)/shard_map/ppermute | solution.py:29
  4.8 34.0 %collective-permute-start.1 = (bf16[128,512]{1,0:T(8,128)(2,1)S(1)}, bf16[128,512]{1,0:T(8,128)(2,1)}, u32[]{:S(2)}, u32[]{:S(2)}) collective-permute-start(bf16[128,512]{1,0:T(8,128)(2,1)S(1)} %fusion.79), channel_id=1, source_target_pairs={{0,2},{1,3},{2,0},{3,1},{4,6},{5,7},{6,4},{7,5},{8,10},{9,11},{10,... | collective-permute-start | bytes 393224 | tf_op jit(solution)/shard_map/ppermute | solution.py:29
  7.4 32.0 %collective-permute-start.5 = (bf16[128,512]{1,0:T(8,128)(2,1)S(1)}, bf16[128,512]{1,0:T(8,128)(2,1)}, u32[]{:S(2)}, u32[]{:S(2)}) collective-permute-start(bf16[128,512]{1,0:T(8,128)(2,1)S(1)} %fusion.79), channel_id=1, source_target_pairs={{0,3},{1,2},{2,1},{3,0},{4,7},{5,6},{6,5},{7,4},{8,11},{9,10},{10,... | collective-permute-start | bytes 393224 | tf_op jit(solution)/shard_map/ppermute | solution.py:29
  9.1 38.9 %collective-permute-start.9 = (bf16[128,1024]{1,0:T(8,128)(2,1)}, bf16[128,1024]{1,0:T(8,128)(2,1)}, u32[]{:S(2)}, u32[]{:S(2)}) collective-permute-start(bf16[128,1024]{1,0:T(8,128)(2,1)} %constant_dynamic-slice_fusion.35), channel_id=1, source_target_pairs={{0,1},{1,0},{2,3},{3,2},{4,5},{5,4},{6,7},{7,6},{8,9},{9,8},{10,11... | collective-permute-start | bytes 786440 | tf_op jit(solution)/shard_map/ppermute | solution.py:29
  10.0 43.8 %collective-permute-start.17 = (bf16[128,1024]{1,0:T(8,128)(2,1)}, bf16[128,1024]{1,0:T(8,128)(2,1)}, u32[]{:S(2)}, u32[]{:S(2)}) collective-permute-start(bf16[128,1024]{1,0:T(8,128)(2,1)} %constant_dynamic-slice_fusion.35), channel_id=1, source_target_pairs={{0,2},{1,3},{2,0},{3,1},{4,6},{5,7},{6,4},{7,5},{8,10},{9,11},{10,... | collective-permute-start | bytes 786440 | tf_op jit(solution)/shard_map/ppermute | solution.py:29
  38.8 25.9 %collective-permute-start.21 = (bf16[128,1024]{1,0:T(8,128)(2,1)}, bf16[128,1024]{1,0:T(8,128)(2,1)S(1)}, u32[]{:S(2)}, u32[]{:S(2)}) collective-permute-start(bf16[128,1024]{1,0:T(8,128)(2,1)} %constant_dynamic-slice_fusion.34), channel_id=1, source_target_pairs={{0,2},{1,3},{2,0},{3,1},{4,6},{5,7},{6,4},{7,5},{8,10},{9,11},{10,... | collective-permute-start | bytes 786440 | tf_op jit(solution)/shard_map/ppermute | solution.py:29
  76.7 24.1 %collective-permute-start.11 = (bf16[2,1,1,128,1024]{4,3,2,1,0:T(8,128)(2,1)S(1)}, bf16[2,1,1,128,1024]{4,3,2,1,0:T(8,128)(2,1)S(1)}, u32[]{:S(2)}, u32[]{:S(2)}) collective-permute-start(bf16[2,1,1,128,1024]{4,3,2,1,0:T(8,128)(2,1)S(1)} %pad_maximum_fusion.35), channel_id=1, source_target_pairs={{0,8},{4,12},{8,0},{12,4},{16,24},{20,28},{24,16},{28,20},{1,9},{5... | collective-permute-start | bytes 1572872 | tf_op jit(solution)/shard_map/ppermute | solution.py:29
  79.7 22.8 %collective-permute-start.15 = (bf16[1,2,1,128,1024]{4,3,2,1,0:T(8,128)(2,1)S(1)}, bf16[1,2,1,128,1024]{4,3,2,1,0:T(8,128)(2,1)S(1)}, u32[]{:S(2)}, u32[]{:S(2)}) collective-permute-start(bf16[1,2,1,128,1024]{4,3,2,1,0:T(8,128)(2,1)S(1)} %pad_maximum_fusion.36), channel_id=1, source_target_pairs={{0,16},{4,20},{8,24},{12,28},{16,0},{20,4},{24,8},{28,12},{1,17},{... | collective-permute-start | bytes 1572872 | tf_op jit(solution)/shard_map/ppermute | solution.py:29
  81.6 27.3 %collective-permute-start.19 = (bf16[2,1,1,128,1024]{4,3,2,1,0:T(8,128)(2,1)S(1)}, bf16[2,1,1,128,1024]{4,3,2,1,0:T(8,128)(2,1)S(1)}, u32[]{:S(2)}, u32[]{:S(2)}) collective-permute-start(bf16[2,1,1,128,1024]{4,3,2,1,0:T(8,128)(2,1)S(1)} %pad_maximum_fusion.37), channel_id=1, source_target_pairs={{0,8},{4,12},{8,0},{12,4},{16,24},{20,28},{24,16},{28,20},{1,9},{5... | collective-permute-start | bytes 1572872 | tf_op jit(solution)/shard_map/ppermute | solution.py:29
  88.2 22.1 %collective-permute-start.23 = (bf16[1,2,1,128,1024]{4,3,2,1,0:T(8,128)(2,1)S(1)}, bf16[1,2,1,128,1024]{4,3,2,1,0:T(8,128)(2,1)S(1)}, u32[]{:S(2)}, u32[]{:S(2)}) collective-permute-start(bf16[1,2,1,128,1024]{4,3,2,1,0:T(8,128)(2,1)S(1)} %pad_maximum_fusion.38), channel_id=1, source_target_pairs={{0,16},{4,20},{8,24},{12,28},{16,0},{20,4},{24,8},{28,12},{1,17},{... | collective-permute-start | bytes 1572872 | tf_op jit(solution)/shard_map/ppermute | solution.py:29
  90.0 24.5 %collective-permute-start.27 = (bf16[2,1,1,128,1024]{4,3,2,1,0:T(8,128)(2,1)S(1)}, bf16[2,1,1,128,1024]{4,3,2,1,0:T(8,128)(2,1)S(1)}, u32[]{:S(2)}, u32[]{:S(2)}) collective-permute-start(bf16[2,1,1,128,1024]{4,3,2,1,0:T(8,128)(2,1)S(1)} %pad_maximum_fusion.39), channel_id=1, source_target_pairs={{0,8},{4,12},{8,0},{12,4},{16,24},{20,28},{24,16},{28,20},{1,9},{5... | collective-permute-start | bytes 1572872 | tf_op jit(solution)/shard_map/ppermute | solution.py:29
  110.2 67.5 %collective-permute-start.12 = (bf16[2,2,1,128,1024]{4,3,2,1,0:T(8,128)(2,1)}, bf16[2,2,1,128,1024]{4,3,2,1,0:T(8,128)(2,1)}, u32[]{:S(2)}, u32[]{:S(2)}) collective-permute-start(bf16[2,2,1,128,1024]{4,3,2,1,0:T(8,128)(2,1)} %pad_maximum_fusion.26), channel_id=1, source_target_pairs={{0,4},{4,0},{8,12},{12,8},{16,20},{20,16},{24,28},{28,24},{1,5},{5... | collective-permute-start | bytes 3145736 | tf_op jit(solution)/shard_map/ppermute | solution.py:29
  114.5 68.1 %collective-permute-start.16 = (bf16[2,2,1,128,1024]{4,3,2,1,0:T(8,128)(2,1)}, bf16[2,2,1,128,1024]{4,3,2,1,0:T(8,128)(2,1)}, u32[]{:S(2)}, u32[]{:S(2)}) collective-permute-start(bf16[2,2,1,128,1024]{4,3,2,1,0:T(8,128)(2,1)} %pad_maximum_fusion.27), channel_id=1, source_target_pairs={{0,4},{4,0},{8,12},{12,8},{16,20},{20,16},{24,28},{28,24},{1,5},{5... | collective-permute-start | bytes 3145736 | tf_op jit(solution)/shard_map/ppermute | solution.py:29
  115.9 64.1 %collective-permute-start.20 = (bf16[2,2,1,128,1024]{4,3,2,1,0:T(8,128)(2,1)}, bf16[2,2,1,128,1024]{4,3,2,1,0:T(8,128)(2,1)}, u32[]{:S(2)}, u32[]{:S(2)}) collective-permute-start(bf16[2,2,1,128,1024]{4,3,2,1,0:T(8,128)(2,1)} %pad_maximum_fusion.28), channel_id=1, source_target_pairs={{0,4},{4,0},{8,12},{12,8},{16,20},{20,16},{24,28},{28,24},{1,5},{5... | collective-permute-start | bytes 3145736 | tf_op jit(solution)/shard_map/ppermute | solution.py:29
  117.8 71.4 %collective-permute-start.24 = (bf16[2,2,1,128,1024]{4,3,2,1,0:T(8,128)(2,1)}, bf16[2,2,1,128,1024]{4,3,2,1,0:T(8,128)(2,1)}, u32[]{:S(2)}, u32[]{:S(2)}) collective-permute-start(bf16[2,2,1,128,1024]{4,3,2,1,0:T(8,128)(2,1)} %pad_maximum_fusion.29), channel_id=1, source_target_pairs={{0,4},{4,0},{8,12},{12,8},{16,20},{20,16},{24,28},{28,24},{1,5},{5... | collective-permute-start | bytes 3145736 | tf_op jit(solution)/shard_map/ppermute | solution.py:29
  118.9 75.9 %collective-permute-start.28 = (bf16[2,2,1,128,1024]{4,3,2,1,0:T(8,128)(2,1)}, bf16[2,2,1,128,1024]{4,3,2,1,0:T(8,128)(2,1)}, u32[]{:S(2)}, u32[]{:S(2)}) collective-permute-start(bf16[2,2,1,128,1024]{4,3,2,1,0:T(8,128)(2,1)} %pad_maximum_fusion.30), channel_id=1, source_target_pairs={{0,4},{4,0},{8,12},{12,8},{16,20},{20,16},{24,28},{28,24},{1,5},{5... | collective-permute-start | bytes 3145736 | tf_op jit(solution)/shard_map/ppermute | solution.py:29
  178.2 21.5 %collective-permute-start.32 = (bf16[2,2,1,128,1024]{4,3,2,1,0:T(8,128)(2,1)S(1)}, bf16[2,2,1,128,1024]{4,3,2,1,0:T(8,128)(2,1)S(1)}, u32[]{:S(2)}, u32[]{:S(2)}) collective-permute-start(bf16[2,2,1,128,1024]{4,3,2,1,0:T(8,128)(2,1)S(1)} %copy-done.79), channel_id=1, source_target_pairs={{0,4},{4,0},{8,12},{12,8},{16,20},{20,16},{24,28},{28,24},{1,5},{5... | collective-permute-start | bytes 3145736 | tf_op jit(solution)/shard_map/ppermute | solution.py:29
  180.1 213.3 %collective-permute-start.66 = (bf16[2,2,1,128,1024]{4,3,2,1,0:T(8,128)(2,1)}, bf16[2,2,1,128,1024]{4,3,2,1,0:T(8,128)(2,1)}, u32[]{:S(2)}, u32[]{:S(2)}) collective-permute-start(bf16[2,2,1,128,1024]{4,3,2,1,0:T(8,128)(2,1)} %constant_dynamic-slice_fusion.13), channel_id=1, source_target_pairs={{0,4},{4,0},{8,12},{12,8},{16,20},{20,16},{24,28},{28,24},{1,5},{5... | collective-permute-start | bytes 3145736 | tf_op jit(solution)/shard_map/ppermute | solution.py:29
  182.6 212.4 %collective-permute-start.51 = (bf16[2,2,1,128,1024]{4,3,2,1,0:T(8,128)(2,1)}, bf16[2,2,1,128,1024]{4,3,2,1,0:T(8,128)(2,1)}, u32[]{:S(2)}, u32[]{:S(2)}) collective-permute-start(bf16[2,2,1,128,1024]{4,3,2,1,0:T(8,128)(2,1)} %constant_dynamic-slice_fusion.25), channel_id=1, source_target_pairs={{0,4},{4,0},{8,12},{12,8},{16,20},{20,16},{24,28},{28,24},{1,5},{5... | collective-permute-start | bytes 3145736 | tf_op jit(solution)/shard_map/ppermute | solution.py:29
  284.6 31.8 %collective-permute-start.81 = (f32[6,1024]{1,0:T(8,128)S(1)}, f32[6,1024]{1,0:T(8,128)S(1)}, u32[]{:S(2)}, u32[]{:S(2)}) collective-permute-start(f32[6,1024]{1,0:T(8,128)S(1)} %stack.27), channel_id=1, source_target_pairs={{0,4},{4,0},{8,12},{12,8},{16,20},{20,16},{24,28},{28,24},{1,5},{5... | collective-permute-start | bytes 73736 | tf_op jit(solution)/shard_map/ppermute | solution.py:29
  335.7 125.6 %collective-permute-start.34 = (bf16[6,64,1024]{2,1,0:T(8,128)(2,1)S(1)}, bf16[6,64,1024]{2,1,0:T(8,128)(2,1)S(1)}, u32[]{:S(2)}, u32[]{:S(2)}) collective-permute-start(bf16[6,64,1024]{2,1,0:T(8,128)(2,1)S(1)} %bitcast.314), channel_id=1, source_target_pairs={{0,2},{1,3},{2,0},{3,1},{4,6},{5,7},{6,4},{7,5},{8,10},{9,11},{10,... | collective-permute-start | bytes 2359304 | tf_op jit(solution)/shard_map/ppermute | solution.py:29
  337.4 34.5 %collective-permute-start.85 = (f32[6,1024]{1,0:T(8,128)S(1)}, f32[6,1024]{1,0:T(8,128)S(1)}, u32[]{:S(2)}, u32[]{:S(2)}) collective-permute-start(f32[6,1024]{1,0:T(8,128)S(1)} %add.450), channel_id=1, source_target_pairs={{0,2},{1,3},{2,0},{3,1},{4,6},{5,7},{6,4},{7,5},{8,10},{9,11},{10,... | collective-permute-start | bytes 73736 | tf_op jit(solution)/shard_map/ppermute | solution.py:29
  340.7 31.9 %collective-permute-start.36 = (bf16[6,16,1024]{2,1,0:T(8,128)(2,1)S(1)}, bf16[6,16,1024]{2,1,0:T(8,128)(2,1)S(1)}, u32[]{:S(2)}, u32[]{:S(2)}) collective-permute-start(bf16[6,16,1024]{2,1,0:T(8,128)(2,1)S(1)} %get-tuple-element.82), channel_id=1, source_target_pairs={{0,1},{1,0},{2,3},{3,2},{4,5},{5,4},{6,7},{7,6},{8,9},{9,8},{10,11... | collective-permute-start | bytes 589832 | tf_op jit(solution)/shard_map/ppermute | solution.py:29
  387.6 74.6 %collective-permute-start.35 = (bf16[6,64,1024]{2,1,0:T(8,128)(2,1)S(1)}, bf16[6,64,1024]{2,1,0:T(8,128)(2,1)S(1)}, u32[]{:S(2)}, u32[]{:S(2)}) collective-permute-start(bf16[6,64,1024]{2,1,0:T(8,128)(2,1)S(1)} %bitcast.315), channel_id=1, source_target_pairs={{0,3},{1,2},{2,1},{3,0},{4,7},{5,6},{6,5},{7,4},{8,11},{9,10},{10,... | collective-permute-start | bytes 2359304 | tf_op jit(solution)/shard_map/ppermute | solution.py:29
  389.0 72.0 %collective-permute-start.33 = (bf16[6,64,1024]{2,1,0:T(8,128)(2,1)S(1)}, bf16[6,64,1024]{2,1,0:T(8,128)(2,1)S(1)}, u32[]{:S(2)}, u32[]{:S(2)}) collective-permute-start(bf16[6,64,1024]{2,1,0:T(8,128)(2,1)S(1)} %bitcast.316), channel_id=1, source_target_pairs={{0,1},{1,0},{2,3},{3,2},{4,5},{5,4},{6,7},{7,6},{8,9},{9,8},{10,11... | collective-permute-start | bytes 2359304 | tf_op jit(solution)/shard_map/ppermute | solution.py:29
  393.4 66.0 %collective-permute-start.39 = (bf16[6,64,1024]{2,1,0:T(8,128)(2,1)S(1)}, bf16[6,64,1024]{2,1,0:T(8,128)(2,1)S(1)}, u32[]{:S(2)}, u32[]{:S(2)}) collective-permute-start(bf16[6,64,1024]{2,1,0:T(8,128)(2,1)S(1)} %get-tuple-element.37), channel_id=1, source_target_pairs={{0,1},{1,0},{2,3},{3,2},{4,5},{5,4},{6,7},{7,6},{8,9},{9,8},{10,11... | collective-permute-start | bytes 2359304 | tf_op jit(solution)/shard_map/ppermute | solution.py:29
  395.1 67.8 %collective-permute-start.40 = (bf16[6,64,1024]{2,1,0:T(8,128)(2,1)S(1)}, bf16[6,64,1024]{2,1,0:T(8,128)(2,1)S(1)}, u32[]{:S(2)}, u32[]{:S(2)}) collective-permute-start(bf16[6,64,1024]{2,1,0:T(8,128)(2,1)S(1)} %get-tuple-element.39), channel_id=1, source_target_pairs={{0,2},{1,3},{2,0},{3,1},{4,6},{5,7},{6,4},{7,5},{8,10},{9,11},{10,... | collective-permute-start | bytes 2359304 | tf_op jit(solution)/shard_map/ppermute | solution.py:29
  459.4 21.4 %collective-permute-start.41 = (bf16[6,64,1024]{2,1,0:T(8,128)(2,1)S(1)}, bf16[6,64,1024]{2,1,0:T(8,128)(2,1)S(1)}, u32[]{:S(2)}, u32[]{:S(2)}) collective-permute-start(bf16[6,64,1024]{2,1,0:T(8,128)(2,1)S(1)} %get-tuple-element.38), channel_id=1, source_target_pairs={{0,3},{1,2},{2,1},{3,0},{4,7},{5,6},{6,5},{7,4},{8,11},{9,10},{10,... | collective-permute-start | bytes 2359304 | tf_op jit(solution)/shard_map/ppermute | solution.py:29
  461.0 33.0 %collective-permute-start.69 = (bf16[2,2,1,128,1024]{4,3,2,1,0:T(8,128)(2,1)S(1)}, bf16[2,2,1,128,1024]{4,3,2,1,0:T(8,128)(2,1)S(1)}, u32[]{:S(2)}, u32[]{:S(2)}) collective-permute-start(bf16[2,2,1,128,1024]{4,3,2,1,0:T(8,128)(2,1)S(1)} %copy-done.73), channel_id=1, source_target_pairs={{0,4},{4,0},{8,12},{12,8},{16,20},{20,16},{24,28},{28,24},{1,5},{5... | collective-permute-start | bytes 3145736 | tf_op jit(solution)/shard_map/ppermute | solution.py:29
  462.2 32.9 %collective-permute-start.73 = (bf16[2,2,1,128,1024]{4,3,2,1,0:T(8,128)(2,1)S(1)}, bf16[2,2,1,128,1024]{4,3,2,1,0:T(8,128)(2,1)S(1)}, u32[]{:S(2)}, u32[]{:S(2)}) collective-permute-start(bf16[2,2,1,128,1024]{4,3,2,1,0:T(8,128)(2,1)S(1)} %copy-done.72), channel_id=1, source_target_pairs={{0,4},{4,0},{8,12},{12,8},{16,20},{20,16},{24,28},{28,24},{1,5},{5... | collective-permute-start | bytes 3145736 | tf_op jit(solution)/shard_map/ppermute | solution.py:29
  462.5 33.5 %collective-permute-start.77 = (bf16[2,2,1,128,1024]{4,3,2,1,0:T(8,128)(2,1)S(1)}, bf16[2,2,1,128,1024]{4,3,2,1,0:T(8,128)(2,1)S(1)}, u32[]{:S(2)}, u32[]{:S(2)}) collective-permute-start(bf16[2,2,1,128,1024]{4,3,2,1,0:T(8,128)(2,1)S(1)} %copy-done.71), channel_id=1, source_target_pairs={{0,4},{4,0},{8,12},{12,8},{16,20},{20,16},{24,28},{28,24},{1,5},{5... | collective-permute-start | bytes 3145736 | tf_op jit(solution)/shard_map/ppermute | solution.py:29
  462.8 24.0 %collective-permute-start.67 = (bf16[1,2,1,128,1024]{4,3,2,1,0:T(8,128)(2,1)S(1)}, bf16[1,2,1,128,1024]{4,3,2,1,0:T(8,128)(2,1)S(1)}, u32[]{:S(2)}, u32[]{:S(2)}) collective-permute-start(bf16[1,2,1,128,1024]{4,3,2,1,0:T(8,128)(2,1)S(1)} %constant_dynamic-slice_fusion.12), channel_id=1, source_target_pairs={{0,16},{4,20},{8,24},{12,28},{16,0},{20,4},{24,8},{28,12},{1,17},{... | collective-permute-start | bytes 1572872 | tf_op jit(solution)/shard_map/ppermute | solution.py:29
  497.3 126.7 %collective-permute-start.68 = (bf16[1,1,1,128,1024]{4,3,2,1,0:T(8,128)(2,1)S(1)}, bf16[1,1,1,128,1024]{4,3,2,1,0:T(8,128)(2,1)S(1)}, u32[]{:S(2)}, u32[]{:S(2)}) collective-permute-start(bf16[1,1,1,128,1024]{4,3,2,1,0:T(8,128)(2,1)S(1)} %constant_dynamic-slice_fusion.11), channel_id=1, source_target_pairs={{0,8},{4,12},{8,0},{12,4},{16,24},{20,28},{24,16},{28,20},{1,9},{5... | collective-permute-start | bytes 786440 | tf_op jit(solution)/shard_map/ppermute | solution.py:29
  499.2 145.0 %collective-permute-start.53 = (bf16[1,1,1,128,1024]{4,3,2,1,0:T(8,128)(2,1)S(1)}, bf16[1,1,1,128,1024]{4,3,2,1,0:T(8,128)(2,1)S(1)}, u32[]{:S(2)}, u32[]{:S(2)}) collective-permute-start(bf16[1,1,1,128,1024]{4,3,2,1,0:T(8,128)(2,1)S(1)} %constant_dynamic-slice_fusion.23), channel_id=1, source_target_pairs={{0,16},{4,20},{8,24},{12,28},{16,0},{20,4},{24,8},{28,12},{1,17},{... | collective-permute-start | bytes 786440 | tf_op jit(solution)/shard_map/ppermute | solution.py:29
  502.2 28.7 %collective-permute-start.74 = (bf16[1,2,1,128,1024]{4,3,2,1,0:T(8,128)(2,1)S(1)}, bf16[1,2,1,128,1024]{4,3,2,1,0:T(8,128)(2,1)S(1)}, u32[]{:S(2)}, u32[]{:S(2)}) collective-permute-start(bf16[1,2,1,128,1024]{4,3,2,1,0:T(8,128)(2,1)S(1)} %constant_dynamic-slice_fusion.6), channel_id=1, source_target_pairs={{0,16},{4,20},{8,24},{12,28},{16,0},{20,4},{24,8},{28,12},{1,17},{... | collective-permute-start | bytes 1572872 | tf_op jit(solution)/shard_map/ppermute | solution.py:29
  503.3 37.8 %collective-permute-start.78 = (bf16[1,2,1,128,1024]{4,3,2,1,0:T(8,128)(2,1)S(1)}, bf16[1,2,1,128,1024]{4,3,2,1,0:T(8,128)(2,1)S(1)}, u32[]{:S(2)}, u32[]{:S(2)}) collective-permute-start(bf16[1,2,1,128,1024]{4,3,2,1,0:T(8,128)(2,1)S(1)} %constant_dynamic-slice_fusion.3), channel_id=1, source_target_pairs={{0,16},{4,20},{8,24},{12,28},{16,0},{20,4},{24,8},{28,12},{1,17},{... | collective-permute-start | bytes 1572872 | tf_op jit(solution)/shard_map/ppermute | solution.py:29
  519.7 22.1 %collective-permute-start.55 = (bf16[2,1,1,128,1024]{4,3,2,1,0:T(8,128)(2,1)S(1)}, bf16[2,1,1,128,1024]{4,3,2,1,0:T(8,128)(2,1)S(1)}, u32[]{:S(2)}, u32[]{:S(2)}) collective-permute-start(bf16[2,1,1,128,1024]{4,3,2,1,0:T(8,128)(2,1)S(1)} %constant_dynamic-slice_fusion.21), channel_id=1, source_target_pairs={{0,8},{4,12},{8,0},{12,4},{16,24},{20,28},{24,16},{28,20},{1,9},{5... | collective-permute-start | bytes 1572872 | tf_op jit(solution)/shard_map/ppermute | solution.py:29
  542.7 24.4 %collective-permute-start.43 = (bf16[2,1,1,128,2,4,128]{6,3,2,1,0,5,4:T(8,128)(2,1)S(1)}, bf16[2,1,1,128,2,4,128]{6,3,2,1,0,5,4:T(8,128)(2,1)S(1)}, u32[]{:S(2)}, u32[]{:S(2)}) collective-permute-start(bf16[2,1,1,128,2,4,128]{6,3,2,1,0,5,4:T(8,128)(2,1)S(1)} %constant_dynamic-slice_fusion.31), channel_id=1, source_target_pairs={{0,8},{4,12},{8,0},{12,4},{16,24},{20,28},{24,16},{28,20},{1,9},{5... | collective-permute-start | bytes 1572872 | tf_op jit(solution)/shard_map/ppermute | solution.py:29
  556.6 21.7 %collective-permute-start.75 = (bf16[1,1,1,128,1024]{4,3,2,1,0:T(8,128)(2,1)S(1)}, bf16[1,1,1,128,1024]{4,3,2,1,0:T(8,128)(2,1)S(1)}, u32[]{:S(2)}, u32[]{:S(2)}) collective-permute-start(bf16[1,1,1,128,1024]{4,3,2,1,0:T(8,128)(2,1)S(1)} %constant_dynamic-slice_fusion.5), channel_id=1, source_target_pairs={{0,8},{4,12},{8,0},{12,4},{16,24},{20,28},{24,16},{28,20},{1,9},{5... | collective-permute-start | bytes 786440 | tf_op jit(solution)/shard_map/ppermute | solution.py:29
  572.7 20.4 %collective-permute-start.56 = (bf16[1,1,1,128,1024]{4,3,2,1,0:T(8,128)(2,1)S(1)}, bf16[1,1,1,128,1024]{4,3,2,1,0:T(8,128)(2,1)S(1)}, u32[]{:S(2)}, u32[]{:S(2)}) collective-permute-start(bf16[1,1,1,128,1024]{4,3,2,1,0:T(8,128)(2,1)S(1)} %constant_dynamic-slice_fusion.20), channel_id=1, source_target_pairs={{0,16},{4,20},{8,24},{12,28},{16,0},{20,4},{24,8},{28,12},{1,17},{... | collective-permute-start | bytes 786440 | tf_op jit(solution)/shard_map/ppermute | solution.py:29
  587.6 20.2 %collective-permute-start.60 = (bf16[1,1,1,128,1024]{4,3,2,1,0:T(8,128)(2,1)S(1)}, bf16[1,1,1,128,1024]{4,3,2,1,0:T(8,128)(2,1)S(1)}, u32[]{:S(2)}, u32[]{:S(2)}) collective-permute-start(bf16[1,1,1,128,1024]{4,3,2,1,0:T(8,128)(2,1)S(1)} %constant_dynamic-slice_fusion.17), channel_id=1, source_target_pairs={{0,16},{4,20},{8,24},{12,28},{16,0},{20,4},{24,8},{28,12},{1,17},{... | collective-permute-start | bytes 786440 | tf_op jit(solution)/shard_map/ppermute | solution.py:29
  592.3 20.3 %collective-permute-start.64 = (bf16[1,1,1,128,1024]{4,3,2,1,0:T(8,128)(2,1)S(1)}, bf16[1,1,1,128,1024]{4,3,2,1,0:T(8,128)(2,1)S(1)}, u32[]{:S(2)}, u32[]{:S(2)}) collective-permute-start(bf16[1,1,1,128,1024]{4,3,2,1,0:T(8,128)(2,1)S(1)} %constant_dynamic-slice_fusion.14), channel_id=1, source_target_pairs={{0,16},{4,20},{8,24},{12,28},{16,0},{20,4},{24,8},{28,12},{1,17},{... | collective-permute-start | bytes 786440 | tf_op jit(solution)/shard_map/ppermute | solution.py:29
  593.1 22.0 %collective-permute-start.48 = (bf16[128,4,128]{2,0,1:T(8,128)(2,1)S(1)}, bf16[128,4,128]{2,0,1:T(8,128)(2,1)S(1)}, u32[]{:S(2)}, u32[]{:S(2)}) collective-permute-start(bf16[128,4,128]{2,0,1:T(8,128)(2,1)S(1)} %get-tuple-element.89), channel_id=1, source_target_pairs={{0,1},{1,0},{2,3},{3,2},{4,5},{5,4},{6,7},{7,6},{8,9},{9,8},{10,11... | collective-permute-start | bytes 393224 | tf_op jit(solution)/shard_map/ppermute | solution.py:29
  618.9 21.3 %collective-permute-start.76 = (bf16[128,1024]{1,0:T(8,128)(2,1)S(1)}, bf16[128,1024]{1,0:T(8,128)(2,1)S(1)}, u32[]{:S(2)}, u32[]{:S(2)}) collective-permute-start(bf16[128,1024]{1,0:T(8,128)(2,1)S(1)} %fusion.69), channel_id=1, source_target_pairs={{0,2},{1,3},{2,0},{3,1},{4,6},{5,7},{6,4},{7,5},{8,10},{9,11},{10,... | collective-permute-start | bytes 786440 | tf_op jit(solution)/shard_map/ppermute | solution.py:29
  621.0 22.2 %collective-permute-start.80 = (bf16[128,1024]{1,0:T(8,128)(2,1)S(1)}, bf16[128,1024]{1,0:T(8,128)(2,1)S(1)}, u32[]{:S(2)}, u32[]{:S(2)}) collective-permute-start(bf16[128,1024]{1,0:T(8,128)(2,1)S(1)} %fusion.70), channel_id=1, source_target_pairs={{0,3},{1,2},{2,1},{3,0},{4,7},{5,6},{6,5},{7,4},{8,11},{9,10},{10,... | collective-permute-start | bytes 786440 | tf_op jit(solution)/shard_map/ppermute | solution.py:29
  624.0 20.2 %collective-permute-start.57 = (bf16[128,1024]{1,0:T(8,128)(2,1)S(1)}, bf16[128,1024]{1,0:T(8,128)(2,1)S(1)}, u32[]{:S(2)}, u32[]{:S(2)}) collective-permute-start(bf16[128,1024]{1,0:T(8,128)(2,1)S(1)} %fusion.65), channel_id=1, source_target_pairs={{0,1},{1,0},{2,3},{3,2},{4,5},{5,4},{6,7},{7,6},{8,9},{9,8},{10,11... | collective-permute-start | bytes 786440 | tf_op jit(solution)/shard_map/ppermute | solution.py:29
  627.2 35.5 %collective-permute-start.61 = (bf16[128,1024]{1,0:T(8,128)(2,1)S(1)}, bf16[128,1024]{1,0:T(8,128)(2,1)S(1)}, u32[]{:S(2)}, u32[]{:S(2)}) collective-permute-start(bf16[128,1024]{1,0:T(8,128)(2,1)S(1)} %fusion.66), channel_id=1, source_target_pairs={{0,2},{1,3},{2,0},{3,1},{4,6},{5,7},{6,4},{7,5},{8,10},{9,11},{10,... | collective-permute-start | bytes 786440 | tf_op jit(solution)/shard_map/ppermute | solution.py:29
  640.2 22.4 %collective-permute-start.65 = (bf16[128,1024]{1,0:T(8,128)(2,1)S(1)}, bf16[128,1024]{1,0:T(8,128)(2,1)S(1)}, u32[]{:S(2)}, u32[]{:S(2)}) collective-permute-start(bf16[128,1024]{1,0:T(8,128)(2,1)S(1)} %fusion.67), channel_id=1, source_target_pairs={{0,3},{1,2},{2,1},{3,0},{4,7},{5,6},{6,5},{7,4},{8,11},{9,10},{10,... | collective-permute-start | bytes 786440 | tf_op jit(solution)/shard_map/ppermute | solution.py:29
  (169 other events, 1045.1 us)
